TPU v7x, 32 devices: a whole 2x2x4 slice. The times are simulated.
32 devices in a mesh: ep: 8 (over z, x), tp: 4 (over y, core).
Axes of the slice: x: 2, y: 2, z: 4, core: 2. Of those that a mesh axis runs over, the one named last changes fastest.
Arguments:
- tokens: bfloat16 [2, 1024, 4096], P(None, 'ep', 'tp'), may hold values from -6 to 6
- expert_ids: int32 [2, 1024, 8], P(None, 'ep'), may hold values from 0 to 31, all different within a row; in each aligned block of 128 rows (0 to 127, 128 to 255, ..., all dimensions but the last counted through in order) at most 40 rows name the same one
- route_weight: float32 [2, 1024, 8], P(None, 'ep'), may hold values from 0.1 to 1
- gate_weight: bfloat16 [32, 1536, 4096], P('ep', 'tp'), may hold values from -0.09375 to 0.09375
- up_weight: bfloat16 [32, 1536, 4096], P('ep', 'tp'), may hold values from -0.09375 to 0.09375
- down_weight: bfloat16 [32, 1536, 4096], P('ep', None, 'tp'), may hold values from -0.15625 to 0.15625
- home_slot: int32 [32], replicated, may hold values from 0 to 31, as said below
- spare_expert: int32 [8], replicated, may hold values from 0 to 31, as said below
Outputs:
- mixed: bfloat16 [2, 1024, 4096], P(None, 'ep', 'tp')
- spare_gate: bfloat16 [8, 1536, 4096], P('ep', 'tp')
- spare_up: bfloat16 [8, 1536, 4096], P('ep', 'tp')
- spare_down: bfloat16 [8, 1536, 4096], P('ep', None, 'tp')
Inputs may be any that keep to these rules, and one draw needn't show every extreme that they name: `home_slot`: a permutation; slot s belongs to ep index s // 4. `spare_expert`: names at most 6 distinct experts, whose home slots lie on distinct ep indices; entry d never names an expert whose home slot lies on ep index d. `expert_ids`: each token names 8 distinct experts; in each micro-step the 128 tokens of one ep index name one expert at most 40 times.
All inputs are finite; a program needn't handle non-finite values.
Results may differ from a plain program's by a relative error of at most 0.0058.
Values may be sent and summed in bfloat16 or wider, within the bound.
No kernel may reach another device: no remote copies, remote signals or barrier semaphores. Data moves between devices by JAX's collectives and lax.ppermute only.
A program may use at most 192 MiB of HBM per device.

v0:
```python
import jax
import jax.numpy as jnp
from jax import lax
from jax.sharding import PartitionSpec as P

TOP = 8
STEPS = 2


def slot_targets(expert_pick, home_slot, capacity):
    count_all = home_slot.shape[0]
    expert_iota = lax.iota(jnp.int32, count_all)
    slot_pick = jnp.sum(jnp.where(expert_pick[..., None] == expert_iota, home_slot, 0), axis=-1)
    pair_shape = expert_pick.shape[:-2] + (expert_pick.shape[-2] * expert_pick.shape[-1],)
    pair_slot = slot_pick.reshape(pair_shape)
    one_hot = (pair_slot[..., None] == expert_iota).astype(jnp.int32)
    earlier = jnp.cumsum(one_hot, axis=-2) - one_hot
    position = jnp.sum(earlier * one_hot, axis=-1)
    return (pair_slot * capacity + position).reshape(expert_pick.shape)


def run_steps(tokens, expert_pick, route_weight, gate_weight, up_weight, down_weight, home_slot):
    batches = tokens.shape[0]
    tok_count = tokens.shape[1]
    width_local = tokens.shape[2]
    experts_all = home_slot.shape[0]
    local_count = gate_weight.shape[0]
    owners = experts_all // local_count
    capacity = tok_count * TOP * 5 // (4 * experts_all)
    slot_rows = local_count * capacity
    total_rows = experts_all * capacity
    own_target = slot_targets(expert_pick, home_slot, capacity)
    placing = jnp.any(own_target[..., None] == lax.iota(jnp.int32, total_rows), axis=2).astype(
        jnp.bfloat16
    )
    outgoing = jnp.einsum(
        "btr,btd->brd", placing, tokens, preferred_element_type=jnp.float32
    ).astype(jnp.bfloat16)
    outgoing = outgoing.reshape(batches, owners, slot_rows, width_local)
    arrived = lax.all_to_all(outgoing, "ep", split_axis=1, concat_axis=1, tiled=True)
    piece = lax.all_gather(arrived, "tp", axis=3, tiled=True)
    piece_rows = piece.reshape(batches, owners, local_count, capacity, piece.shape[3])
    gate_add = jnp.einsum(
        "bsecd,efd->bsecf", piece_rows, gate_weight, preferred_element_type=jnp.float32
    )
    up_add = jnp.einsum(
        "bsecd,efd->bsecf", piece_rows, up_weight, preferred_element_type=jnp.float32
    )
    hidden = (jax.nn.silu(gate_add) * up_add).astype(jnp.bfloat16)
    results = jnp.einsum(
        "bsecf,efd->bsecd",
        lax.all_gather(hidden, "tp", axis=4, tiled=True),
        down_weight,
        preferred_element_type=jnp.float32,
    ).astype(jnp.bfloat16)
    results = results.reshape(batches, owners, slot_rows, width_local)
    returned = lax.all_to_all(results, "ep", split_axis=1, concat_axis=1, tiled=True)
    returned = returned.reshape(batches, total_rows, width_local)
    flat_target = own_target.reshape(batches, tok_count * own_target.shape[2])
    picked_rows = jnp.take_along_axis(returned, flat_target[..., None], axis=1)
    picked_rows = picked_rows.reshape(batches, tok_count, own_target.shape[2], width_local).astype(
        jnp.float32
    )
    mixed = jnp.sum(picked_rows * route_weight[..., None], axis=2)
    return mixed.astype(jnp.bfloat16)


def move_spares(gate_weight, up_weight, down_weight, home_slot, spare_expert):
    local_count = gate_weight.shape[0]
    experts_all = home_slot.shape[0]
    owners = spare_expert.shape[0]
    own_index = lax.axis_index("ep")
    expert_iota = lax.iota(jnp.int32, experts_all)
    spare_slot = jnp.sum(jnp.where(spare_expert[:, None] == expert_iota, home_slot, 0), axis=1)
    spare_home = spare_slot // local_count
    own_slot = jnp.max(jnp.where(spare_home == own_index, spare_slot % local_count, 0))
    gate_part = lax.dynamic_index_in_dim(gate_weight, own_slot, 0, keepdims=False)
    up_part = lax.dynamic_index_in_dim(up_weight, own_slot, 0, keepdims=False)
    down_part = lax.dynamic_index_in_dim(down_weight, own_slot, 0, keepdims=False)
    gate_pieces = gate_part.reshape(gate_part.shape[0], owners, gate_part.shape[1] // owners)
    up_pieces = up_part.reshape(up_part.shape[0], owners, up_part.shape[1] // owners)
    down_pieces = down_part.reshape(down_part.shape[0], owners, down_part.shape[1] // owners)
    spread_gate, spread_up, spread_down = (
        lax.all_to_all(gate_pieces, "ep", split_axis=1, concat_axis=1, tiled=True),
        lax.all_to_all(up_pieces, "ep", split_axis=1, concat_axis=1, tiled=True),
        lax.all_to_all(down_pieces, "ep", split_axis=1, concat_axis=1, tiled=True),
    )
    chosen_gate = jnp.take(spread_gate, spare_home, axis=1)
    chosen_up = jnp.take(spread_up, spare_home, axis=1)
    chosen_down = jnp.take(spread_down, spare_home, axis=1)
    landed_gate, landed_up, landed_down = (
        lax.all_to_all(chosen_gate, "ep", split_axis=1, concat_axis=1, tiled=True),
        lax.all_to_all(chosen_up, "ep", split_axis=1, concat_axis=1, tiled=True),
        lax.all_to_all(chosen_down, "ep", split_axis=1, concat_axis=1, tiled=True),
    )
    spare_gate = landed_gate.reshape(1, gate_part.shape[0], gate_part.shape[1])
    spare_up = landed_up.reshape(1, up_part.shape[0], up_part.shape[1])
    spare_down = landed_down.reshape(1, down_part.shape[0], down_part.shape[1])
    return (spare_gate, spare_up, spare_down)


def shards(
    tokens, expert_ids, route_weight, gate_weight, up_weight, down_weight, home_slot, spare_expert
):
    spare_gate, spare_up, spare_down = move_spares(
        gate_weight, up_weight, down_weight, home_slot, spare_expert
    )
    outputs = [
        run_steps(
            tokens[step_index : step_index + 1],
            expert_ids[step_index : step_index + 1],
            route_weight[step_index : step_index + 1],
            gate_weight,
            up_weight,
            down_weight,
            home_slot,
        )
        for step_index in range(STEPS)
    ]
    mixed = jnp.concatenate(outputs, axis=0)
    return (mixed, spare_gate, spare_up, spare_down)


def solution(mesh):
    placed = (
        P(None, "ep", "tp"),
        P(None, "ep", None),
        P(None, "ep", None),
        P("ep", "tp", None),
        P("ep", "tp", None),
        P("ep", None, "tp"),
        P(),
        P(),
    )
    return jax.shard_map(
        shards,
        mesh=mesh,
        in_specs=placed,
        out_specs=(
            P(None, "ep", "tp"),
            P("ep", "tp", None),
            P("ep", "tp", None),
            P("ep", None, "tp"),
        ),
        check_vma=False,
    )
```

profile of v0, /device:TPU:0, one launch (start us, length us, event | category | flops | bytes accessed | tf_op | source)
XLA Modules:
  0.0 761.4 jit_solution(297695629966626307)
XLA Ops:
  7.2 0.8 slice_bitcast_fusion.3
  8.0 0.8 select_reduce_fusion.1
  9.0 9.0 %reduce-window.14 = s32[1,32,8,128]{3,2,1,0:T(8,128)S(1)} reduce-window(s32[1,32,8,128]{3,2,1,0:T(8,128)S(1)} %bitcast.226, s32[]{:T(128)} %constant.82.clone.1), window={size=1x1x1x128 pad=0_0x0_0x0_0x127_0}, to_apply=%region_1.2 | reduce-window | flops 4161536 | bytes 262148 | tf_op jit(solution)/shard_map/reduce-window
  18.4 9.0 %reduce-window.16 = s32[1,32,8,128]{3,2,1,0:T(8,128)S(1)} reduce-window(s32[1,32,8,128]{3,2,1,0:T(8,128)S(1)} %bitcast.227, s32[]{:T(128)} %constant.82.clone.1), window={size=1x1x1x128 pad=0_0x0_0x0_0x127_0}, to_apply=%region_7.9 | reduce-window | flops 4161536 | bytes 262148 | tf_op jit(solution)/shard_map/reduce-window.2
  28.8 1.6 fusion.16
  30.5 0.9 convolution_convert_fusion.1
  31.4 66.7 %all_to_all.50 = bf16[1,8,160,1024]{3,2,0,1:T(8,128)(2,1)} all-to-all(bf16[1,8,160,1024]{3,2,0,1:T(8,128)(2,1)S(1)} %bitcast.223), channel_id=1, replica_groups=mesh['ep'=8,'tp'=4] {'ep'}, dimensions={1} | all-to-all | bytes 5242880 | tf_op jit(solution)/shard_map/all_to_all | solution.py:40
  98.2 1.6 fusion.17
  99.8 2.4 convolution_convert_fusion
  102.2 4.6 all-to-all-start.2
  107.0 0.6 compare_select_fusion.2
  109.7 6.8 constant_dynamic-slice_fusion.1
  116.4 3.4 copy.129
  119.9 2.9 copy.115
  122.7 42.7 %all-to-all-done.2 = bf16[1,8,160,1024]{3,2,0,1:T(8,128)(2,1)} async-done(((bf16[1,8,160,1024]{3,2,0,1:T(8,128)(2,1)}), bf16[1,8,160,1024]{3,2,0,1:T(8,128)(2,1)}, u32[]{:S(2)}, u32[]{:S(2)}) %all-to-all-start.2) | async-done | bytes 2621472 | tf_op jit(solution)/shard_map/all_to_all | solution.py:40
  165.4 3.7 all-to-all-start.4
  169.0 4.6 copy.130
  173.7 4.6 copy.118
  178.3 61.6 %all-to-all-done.4 = bf16[384,8,512]{2,0,1:T(8,128)(2,1)S(1)} async-done(((bf16[384,8,512]{2,0,1:T(8,128)(2,1)}), bf16[384,8,512]{2,0,1:T(8,128)(2,1)S(1)}, u32[]{:S(2)}, u32[]{:S(2)}) %all-to-all-start.4) | async-done | bytes 3145760 | tf_op jit(solution)/shard_map/all_to_all | solution.py:84
  239.9 1.7 copy-done.2
  241.6 4.5 all-to-all-start.6
  246.1 0.7 all-gather.9.cloned.1.call-update
  246.8 2.2 constant_dynamic-slice_fusion
  249.0 2.9 copy.131
  251.9 4.6 copy.121
  256.5 59.7 %all-to-all-done.6 = bf16[384,8,512]{2,0,1:T(8,128)(2,1)} async-done(((bf16[384,8,512]{2,0,1:T(8,128)(2,1)}), bf16[384,8,512]{2,0,1:T(8,128)(2,1)}, u32[]{:S(2)}, u32[]{:S(2)}) %all-to-all-start.6) | async-done | bytes 3145760 | tf_op jit(solution)/shard_map/all_to_all | solution.py:85
  316.2 3.6 all-to-all-start.8
  319.9 4.3 gather_fusion.3
  324.2 4.3 gather_fusion.4
  328.5 6.2 select_bitcast_fusion
  334.6 56.1 %all-to-all-done.8 = bf16[1536,8,128]{2,0,1:T(8,128)(2,1)S(1)} async-done(((bf16[1536,8,128]{2,0,1:T(8,128)(2,1)}), bf16[1536,8,128]{2,0,1:T(8,128)(2,1)S(1)}, u32[]{:S(2)}, u32[]{:S(2)}) %all-to-all-start.8) | async-done | bytes 3145760 | tf_op jit(solution)/shard_map/all_to_all | solution.py:86
  390.7 74.8 %all_to_all.51 = bf16[384,8,512]{2,0,1:T(8,128)(2,1)} all-to-all(bf16[384,8,512]{2,0,1:T(8,128)(2,1)} %get-tuple-element.35), channel_id=1, replica_groups=mesh['ep'=8,'tp'=4] {'ep'}, dimensions={1} | all-to-all | bytes 6291456 | tf_op jit(solution)/shard_map/all_to_all | solution.py:92
  465.5 3.7 all-to-all-start.7
  469.2 0.5 all-gather.7.cloned.1.call-start
  469.7 15.1 %fusion.10 = f32[4,8,40,384]{3,2,1,0:T(8,128)} fusion(bf16[4,384,4096]{2,1,0:T(8,128)(2,1)} %param.15, bf16[8,4,40,4096]{3,2,1,0:T(8,128)(2,1)} %bitcast.234), kind=kOutput, calls=%fused_computation.15 | convolution fusion | flops 4026531840 | bytes 25034752 | tf_op jit(solution)/shard_map/bsecd,efd->bsecf/dot_general | solution.py:43
  484.8 15.3 %fusion.31 = bf16[1,8,4,40,384]{4,3,1,2,0:T(8,128)(2,1)} fusion(f32[4,8,40,384]{3,2,1,0:T(8,128)} %fusion.10, bf16[4,384,4096]{2,1,0:T(8,128)(2,1)} %param.16, bf16[8,4,40,4096]{3,2,1,0:T(8,128)(2,1)} %bitcast.235), kind=kOutput, calls=%fused_computation.43 | convolution fusion | flops 4029480960 | bytes 26017792 | tf_op jit(solution)/shard_map/bsecd,efd->bsecf/dot_general | solution.py:46
  500.2 4.5 gather_fusion
  504.7 3.9 select_bitcast_fusion.2
  508.6 30.7 %all-to-all-done.7 = bf16[384,8,512]{2,0,1:T(8,128)(2,1)S(1)} async-done(((bf16[384,8,512]{2,0,1:T(8,128)(2,1)}), bf16[384,8,512]{2,0,1:T(8,128)(2,1)S(1)}, u32[]{:S(2)}, u32[]{:S(2)}) %all-to-all-start.7) | async-done | bytes 3145760 | tf_op jit(solution)/shard_map/all_to_all | solution.py:93
  539.3 1.7 copy-done
  540.9 4.4 all-to-all-start.9
  545.4 0.2 all-gather.11.cloned.1.call-start
  545.6 14.2 %fusion.8 = f32[4,8,40,384]{3,2,1,0:T(8,128)S(1)} fusion(bf16[4,384,4096]{2,1,0:T(8,128)(2,1)} %param.15, bf16[8,4,40,4096]{3,2,1,0:T(8,128)(2,1)} %bitcast.236), kind=kOutput, calls=%fused_computation.13 | convolution fusion | flops 4026531840 | bytes 25034752 | tf_op jit(solution)/shard_map/bsecd,efd->bsecf/dot_general | solution.py:43
  559.8 15.0 %fusion.30 = bf16[1,8,4,40,384]{4,3,1,2,0:T(8,128)(2,1)} fusion(f32[4,8,40,384]{3,2,1,0:T(8,128)S(1)} %fusion.8, bf16[4,384,4096]{2,1,0:T(8,128)(2,1)} %param.16, bf16[8,4,40,4096]{3,2,1,0:T(8,128)(2,1)} %bitcast.237), kind=kOutput, calls=%fused_computation.41 | convolution fusion | flops 4029480960 | bytes 26017792 | tf_op jit(solution)/shard_map/bsecd,efd->bsecf/dot_general | solution.py:46
  574.9 10.0 %convert_bitcast_fusion.1 = bf16[1,8,4,40,1024]{4,3,1,2,0:T(8,128)(2,1)S(1)} fusion(bf16[4,1536,1024]{2,1,0:T(8,128)(2,1)} %param.17, bf16[1,8,4,40,1536]{4,3,1,2,0:T(8,128)(2,1)} %all-gather.7.cloned.1.call-done), kind=kOutput, calls=%fused_computation.37 | convolution fusion | flops 4027842560 | bytes 19136512 | tf_op jit(solution)/shard_map/bsecf,efd->bsecd/dot_general | solution.py:50
  584.9 1.8 copy.98
  586.7 28.9 %all-to-all-done.9 = bf16[1536,8,128]{2,0,1:T(8,128)(2,1)} async-done(((bf16[1536,8,128]{2,0,1:T(8,128)(2,1)}), bf16[1536,8,128]{2,0,1:T(8,128)(2,1)}, u32[]{:S(2)}, u32[]{:S(2)}) %all-to-all-start.9) | async-done | bytes 3145760 | tf_op jit(solution)/shard_map/all_to_all | solution.py:94
  615.6 3.9 all-to-all-start.1
  619.5 10.0 %convert_bitcast_fusion = bf16[1,8,4,40,1024]{4,3,1,2,0:T(8,128)(2,1)S(1)} fusion(bf16[4,1536,1024]{2,1,0:T(8,128)(2,1)} %param.17, bf16[1,8,4,40,1536]{4,3,1,2,0:T(8,128)(2,1)} %all-gather.11.cloned.1.call-done), kind=kOutput, calls=%fused_computation.36 | convolution fusion | flops 4027842560 | bytes 19136512 | tf_op jit(solution)/shard_map/bsecf,efd->bsecd/dot_general | solution.py:50
  629.5 1.8 copy.111
  631.3 47.8 %all-to-all-done.1 = bf16[1,8,160,1024]{3,2,0,1:T(8,128)(2,1)S(1)} async-done(((bf16[1,8,160,1024]{3,2,0,1:T(8,128)(2,1)}), bf16[1,8,160,1024]{3,2,0,1:T(8,128)(2,1)S(1)}, u32[]{:S(2)}, u32[]{:S(2)}) %all-to-all-start.1) | async-done | bytes 2621472 | tf_op jit(solution)/shard_map/all_to_all | solution.py:57
  679.0 4.4 all-to-all-start.3
  684.1 4.6 copy.116
  688.8 4.6 copy.123
  693.4 4.6 copy.119
  698.0 4.6 copy.124
  702.7 4.6 copy.122
  707.3 4.6 copy.125
  711.9 5.4 gather_fusion.1
  717.3 25.1 %all-to-all-done.3 = bf16[1,8,160,1024]{3,2,0,1:T(8,128)(2,1)} async-done(((bf16[1,8,160,1024]{3,2,0,1:T(8,128)(2,1)}), bf16[1,8,160,1024]{3,2,0,1:T(8,128)(2,1)}, u32[]{:S(2)}, u32[]{:S(2)}) %all-to-all-start.3) | async-done | bytes 2621472 | tf_op jit(solution)/shard_map/all_to_all | solution.py:57
  742.4 8.2 %gather_fusion.2 = bf16[1024,1024]{1,0:T(8,128)(2,1)} fusion(bf16[1280,1024]{1,0:T(8,128)(2,1)} %bitcast.67, s32[1024]{0:T(1024)S(1)} %broadcast_clamp_fusion), kind=kCustom, calls=%fused_computation.2.clone | custom fusion | bytes 4198400 | tf_op jit(solution)/shard_map/jit(take_along_axis)/gather | solution.py:60
  750.7 1.5 fusion.19
  752.3 1.5 fusion.18
  753.8 0.8 pad_maximum_fusion
  (74 shorter events, 3.2 us)
Async XLA Ops:
  7.2 23.3 %copy-start.5 = (bf16[2,128,1024]{2,1,0:T(8,128)(2,1)S(1)}, bf16[2,128,1024]{2,1,0:T(8,128)(2,1)}, u32[]{:S(2)}) copy-start(bf16[2,128,1024]{2,1,0:T(8,128)(2,1)} %param.12) | copy-start | bytes 1572868
  7.2 462.5 %all-gather.5.cloned.1.call-start = ((), (), s32[]{:S(2)}) async-start(), calls=%async_computation.10 | async-start | bytes 13107200 | tf_op jit(solution)/shard_map/all_gather | solution.py:41
  102.2 4.6 copy-start.7
  102.2 4.6 copy-start.8
  102.2 63.2 %all-to-all-start.2 = ((bf16[1,8,160,1024]{3,2,0,1:T(8,128)(2,1)}), bf16[1,8,160,1024]{3,2,0,1:T(8,128)(2,1)}, u32[]{:S(2)}, u32[]{:S(2)}) async-start(bf16[1,8,160,1024]{3,2,0,1:T(8,128)(2,1)} %bitcast.46), calls=%async_computation.2 | async-start | bytes 5242880 | tf_op jit(solution)/shard_map/all_to_all | solution.py:40
  165.4 74.5 %all-to-all-start.4 = ((bf16[384,8,512]{2,0,1:T(8,128)(2,1)}), bf16[384,8,512]{2,0,1:T(8,128)(2,1)S(1)}, u32[]{:S(2)}, u32[]{:S(2)}) async-start(bf16[384,8,512]{2,0,1:T(8,128)(2,1)} %copy.115), calls=%async_computation.4 | async-start | bytes 6291456 | tf_op jit(solution)/shard_map/all_to_all | solution.py:84
  239.9 1.7 copy-start.2
  241.6 74.6 %all-to-all-start.6 = ((bf16[384,8,512]{2,0,1:T(8,128)(2,1)}), bf16[384,8,512]{2,0,1:T(8,128)(2,1)}, u32[]{:S(2)}, u32[]{:S(2)}) async-start(bf16[384,8,512]{2,0,1:T(8,128)(2,1)} %copy.118), calls=%async_computation.6 | async-start | bytes 6291456 | tf_op jit(solution)/shard_map/all_to_all | solution.py:85
  246.0 299.6 %all-gather.9.cloned.1.call-start = ((), (), s32[]{:S(2)}) async-start(), calls=%async_computation.12 | async-start | bytes 13107200 | tf_op jit(solution)/shard_map/all_gather | solution.py:41
  316.2 74.5 %all-to-all-start.8 = ((bf16[1536,8,128]{2,0,1:T(8,128)(2,1)}), bf16[1536,8,128]{2,0,1:T(8,128)(2,1)S(1)}, u32[]{:S(2)}, u32[]{:S(2)}) async-start(bf16[1536,8,128]{2,0,1:T(8,128)(2,1)} %copy.121), calls=%async_computation.8 | async-start | bytes 6291456 | tf_op jit(solution)/shard_map/all_to_all | solution.py:86
  390.7 74.8 %copy-start.1 = (bf16[1536,8,128]{2,0,1:T(8,128)(2,1)}, bf16[1536,8,128]{2,0,1:T(8,128)(2,1)S(1)}, u32[]{:S(2)}) copy-start(bf16[1536,8,128]{2,0,1:T(8,128)(2,1)S(1)} %all-to-all-done.8) | copy-start | bytes 9437188
  465.5 73.8 %all-to-all-start.7 = ((bf16[384,8,512]{2,0,1:T(8,128)(2,1)}), bf16[384,8,512]{2,0,1:T(8,128)(2,1)S(1)}, u32[]{:S(2)}, u32[]{:S(2)}) async-start(bf16[384,8,512]{2,0,1:T(8,128)(2,1)} %get-tuple-element.34), calls=%async_computation.7 | async-start | bytes 6291456 | tf_op jit(solution)/shard_map/all_to_all | solution.py:93
  469.2 105.7 %all-gather.7.cloned.1.call-start = ((), (), s32[]{:S(2)}) async-start(), calls=%async_computation.11 | async-start | bytes 4915200 | tf_op jit(solution)/shard_map/all_gather | solution.py:52
  539.2 1.7 copy-start
  540.9 74.6 %all-to-all-start.9 = ((bf16[1536,8,128]{2,0,1:T(8,128)(2,1)}), bf16[1536,8,128]{2,0,1:T(8,128)(2,1)}, u32[]{:S(2)}, u32[]{:S(2)}) async-start(bf16[1536,8,128]{2,0,1:T(8,128)(2,1)} %select_bitcast_fusion.2), calls=%async_computation.9 | async-start | bytes 6291456 | tf_op jit(solution)/shard_map/all_to_all | solution.py:94
  545.4 74.1 %all-gather.11.cloned.1.call-start = ((), (), s32[]{:S(2)}) async-start(), calls=%async_computation.13 | async-start | bytes 4915200 | tf_op jit(solution)/shard_map/all_gather | solution.py:52
  615.6 63.5 %all-to-all-start.1 = ((bf16[1,8,160,1024]{3,2,0,1:T(8,128)(2,1)}), bf16[1,8,160,1024]{3,2,0,1:T(8,128)(2,1)S(1)}, u32[]{:S(2)}, u32[]{:S(2)}) async-start(bf16[1,8,160,1024]{3,2,0,1:T(8,128)(2,1)} %bitcast.222), calls=%async_computation.1 | async-start | bytes 5242880 | tf_op jit(solution)/shard_map/all_to_all | solution.py:57
  631.3 52.4 %copy-start.6 = (f32[2,128,8]{1,2,0:T(8,128)S(1)}, f32[2,128,8]{1,2,0:T(8,128)}, u32[]{:S(2)}) copy-start(f32[2,128,8]{1,2,0:T(8,128)} %param.14) | copy-start | bytes 24580
  679.0 63.4 %all-to-all-start.3 = ((bf16[1,8,160,1024]{3,2,0,1:T(8,128)(2,1)}), bf16[1,8,160,1024]{3,2,0,1:T(8,128)(2,1)}, u32[]{:S(2)}, u32[]{:S(2)}) async-start(bf16[1,8,160,1024]{3,2,0,1:T(8,128)(2,1)} %bitcast.221), calls=%async_computation.3 | async-start | bytes 5242880 | tf_op jit(solution)/shard_map/all_to_all | solution.py:57
  742.4 8.2 %copy-start.3 = (bf16[1024,1024]{1,0:T(8,128)(2,1)S(1)}, bf16[1024,1024]{1,0:T(8,128)(2,1)}, u32[]{:S(2)}) copy-start(bf16[1024,1024]{1,0:T(8,128)(2,1)} %gather_fusion.1) | copy-start | bytes 6291460
  750.7 1.6 copy-start.4
Sparse Core Ops, SparseCore 0:
  98.2 69.1 all-gather.4
  248.4 71.4 all-gather.8
  500.2 34.2 all-gather.6
  575.0 34.2 all-gather.10
where the time goes:
time: 771 us; the launch traced here: 761 us
  waiting for transfers between devices  353 us (46%)
  blocking collectives  141 us (18%)
  local copies, waits for them, and re-layouts  96.8 us (13%)
  matrix products  82.9 us (11%)
  other arithmetic  37.1 us (5%)
  starting transfers between devices  33.5 us (4%)
  between operations  16.4 us (2%)
    all_to_all x1, blocking collectives, move_spares(): lax.all_to_all(chosen_gate, 'ep', split_axis=1, concat_axis=1, tiled=True)  74.8 us
    all_to_all x2, waiting for transfers between devices, run_steps(): lax.all_to_all(results, 'ep', split_axis=1, concat_axis=1, tiled=True)  72.9 us
    all_to_all x1, blocking collectives, run_steps(): lax.all_to_all(outgoing, 'ep', split_axis=1, concat_axis=1, tiled=True)  66.7 us
    all_to_all x1, waiting for transfers between devices, move_spares(): lax.all_to_all(gate_pieces, 'ep', split_axis=1, concat_axis=1, tiled=True)  61.6 us
    all_to_all x1, waiting for transfers between devices, move_spares(): lax.all_to_all(up_pieces, 'ep', split_axis=1, concat_axis=1, tiled=True)  59.7 us
    all_to_all x1, waiting for transfers between devices, move_spares(): lax.all_to_all(down_pieces, 'ep', split_axis=1, concat_axis=1, tiled=True)  56.1 us
    all_to_all x1, waiting for transfers between devices, run_steps(): lax.all_to_all(outgoing, 'ep', split_axis=1, concat_axis=1, tiled=True)  42.7 us
    all_to_all x1, waiting for transfers between devices, move_spares(): lax.all_to_all(chosen_up, 'ep', split_axis=1, concat_axis=1, tiled=True)  30.7 us
  transfers between devices with their start and end apart: 12, of which 8 were waited for; matrix products, arithmetic and copies ran while one was open for 23% of the time, Pallas kernels for 0%

commit v1 on v0

--- a/solution.py
+++ b/solution.py
@@ -5,6 +5,28 @@
 
 TOP = 8
 STEPS = 2
+
+
+def split_up(value, dim, peers):
+    before, after = (value.shape[:dim], value.shape[dim + 1 :])
+    return jnp.moveaxis(value.reshape(*before, peers, -1, *after), dim, 0)
+
+
+def joined_along(blocks, dim):
+    shape = list(blocks.shape[1:])
+    shape[dim] *= blocks.shape[0]
+    return jnp.moveaxis(blocks, 0, dim).reshape(shape)
+
+
+def pairwise_exchange(x, axis, split_dim, concat_dim):
+    devices, mine = (lax.axis_size(axis), lax.axis_index(axis))
+    blocks = split_up(x, split_dim, devices)
+    outs = [blocks[mine]]
+    for step in range(1, devices):
+        sent = blocks[mine ^ step]
+        outs.append(lax.ppermute(sent, axis, [(i, i ^ step) for i in range(devices)]))
+    blocks = jnp.stack(outs)[mine ^ jnp.arange(devices)]
+    return joined_along(blocks, concat_dim)
 
 
 def slot_targets(expert_pick, home_slot, capacity):
@@ -89,7 +111,7 @@
     chosen_up = jnp.take(spread_up, spare_home, axis=1)
     chosen_down = jnp.take(spread_down, spare_home, axis=1)
     landed_gate, landed_up, landed_down = (
-        lax.all_to_all(chosen_gate, "ep", split_axis=1, concat_axis=1, tiled=True),
+        pairwise_exchange(chosen_gate, "ep", 1, 1),
         lax.all_to_all(chosen_up, "ep", split_axis=1, concat_axis=1, tiled=True),
         lax.all_to_all(chosen_down, "ep", split_axis=1, concat_axis=1, tiled=True),
     )

time: 771 us -> 803 us (1.042)
  the two profiles are of different devices: /device:TPU:0 before, /device:TPU:8 now
where the time goes in v1:
time: 803 us; the launch traced here: 793 us
  waiting for transfers between devices  408 us (51%)
  local copies, waits for them, and re-layouts  115 us (14%)
  matrix products  82.9 us (10%)
  starting transfers between devices  68.2 us (8%)
  blocking collectives  64.7 us (8%)
  other arithmetic  38.2 us (5%)
  between operations  16.4 us (2%)
    ppermute x7, waiting for transfers between devices, pairwise_exchange(): lax.ppermute(sent, axis, [(i, i ^ step) for i in range(devices)])  95.9 us
    all_to_all x1, blocking collectives, run_steps(): lax.all_to_all(outgoing, 'ep', split_axis=1, concat_axis=1, tiled=True)  64.7 us
    all_to_all x1, waiting for transfers between devices, move_spares(): lax.all_to_all(up_pieces, 'ep', split_axis=1, concat_axis=1, tiled=True)  58.4 us
    all_to_all x1, waiting for transfers between devices, move_spares(): lax.all_to_all(gate_pieces, 'ep', split_axis=1, concat_axis=1, tiled=True)  58 us
    all_to_all x1, waiting for transfers between devices, move_spares(): lax.all_to_all(down_pieces, 'ep', split_axis=1, concat_axis=1, tiled=True)  53.7 us
    all_to_all x2, waiting for transfers between devices, run_steps(): lax.all_to_all(results, 'ep', split_axis=1, concat_axis=1, tiled=True)  45.3 us
    all_to_all x1, waiting for transfers between devices, run_steps(): lax.all_to_all(outgoing, 'ep', split_axis=1, concat_axis=1, tiled=True)  40.2 us
    unnamed x37, local copies, waits for them, and re-layouts  38.4 us
  transfers between devices with their start and end apart: 19, of which 14 were waited for; matrix products, arithmetic and copies ran while one was open for 25% of the time, Pallas kernels for 0%

profile of v1, /device:TPU:8, one launch (start us, length us, event | category | flops | bytes accessed | tf_op | source)
XLA Modules:
  0.0 793.0 jit_solution(11217073897088997112)
XLA Ops:
  9.0 9.0 %reduce-window.16 = s32[1,32,8,128]{3,2,1,0:T(8,128)S(1)} reduce-window(s32[1,32,8,128]{3,2,1,0:T(8,128)S(1)} %bitcast.249, s32[]{:T(128)} %constant.68.clone.1), window={size=1x1x1x128 pad=0_0x0_0x0_0x127_0}, to_apply=%region_7.9 | reduce-window | flops 4161536 | bytes 262148 | tf_op jit(solution)/shard_map/reduce-window.2
  18.4 9.0 %reduce-window.14 = s32[1,32,8,128]{3,2,1,0:T(8,128)S(1)} reduce-window(s32[1,32,8,128]{3,2,1,0:T(8,128)S(1)} %bitcast.250, s32[]{:T(128)} %constant.68.clone.1), window={size=1x1x1x128 pad=0_0x0_0x0_0x127_0}, to_apply=%region_1.2 | reduce-window | flops 4161536 | bytes 262148 | tf_op jit(solution)/shard_map/reduce-window
  31.4 64.7 %all_to_all.45 = bf16[1,8,160,1024]{3,2,0,1:T(8,128)(2,1)} all-to-all(bf16[1,8,160,1024]{3,2,0,1:T(8,128)(2,1)S(1)} %bitcast.246), channel_id=1, replica_groups=mesh['ep'=8,'tp'=4] {'ep'}, dimensions={1} | all-to-all | bytes 5242880 | tf_op jit(solution)/shard_map/all_to_all | solution.py:62
  97.8 2.4 convolution_convert_fusion.1
  100.2 5.4 all-to-all-start
  108.5 6.8 constant_dynamic-slice_fusion
  115.3 3.4 copy.132
  118.7 2.9 copy.120
  121.5 40.2 %all-to-all-done = bf16[1,8,160,1024]{3,2,0,1:T(8,128)(2,1)} async-done(((bf16[1,8,160,1024]{3,2,0,1:T(8,128)(2,1)}), bf16[1,8,160,1024]{3,2,0,1:T(8,128)(2,1)}, u32[]{:S(2)}, u32[]{:S(2)}) %all-to-all-start) | async-done | bytes 2621472 | tf_op jit(solution)/shard_map/all_to_all | solution.py:62
  161.8 6.2 all-to-all-start.5
  168.7 4.6 copy.131
  173.3 4.6 copy.117
  178.0 58.4 %all-to-all-done.5 = bf16[384,8,512]{2,0,1:T(8,128)(2,1)S(1)} async-done(((bf16[384,8,512]{2,0,1:T(8,128)(2,1)}), bf16[384,8,512]{2,0,1:T(8,128)(2,1)S(1)}, u32[]{:S(2)}, u32[]{:S(2)}) %all-to-all-start.5) | async-done | bytes 3145760 | tf_op jit(solution)/shard_map/all_to_all | solution.py:107
  236.4 1.7 copy-done.2
  238.1 6.8 all-to-all-start.4
  244.8 2.2 constant_dynamic-slice_fusion.9
  247.0 2.9 copy.133
  250.0 4.6 copy.123
  254.6 58.0 %all-to-all-done.4 = bf16[384,8,512]{2,0,1:T(8,128)(2,1)} async-done(((bf16[384,8,512]{2,0,1:T(8,128)(2,1)}), bf16[384,8,512]{2,0,1:T(8,128)(2,1)}, u32[]{:S(2)}, u32[]{:S(2)}) %all-to-all-start.4) | async-done | bytes 3145760 | tf_op jit(solution)/shard_map/all_to_all | solution.py:106
  312.6 6.2 all-to-all-start.7
  318.8 4.3 gather_fusion.5
  323.1 4.3 gather_fusion.4
  327.4 6.2 select_bitcast_fusion
  333.6 53.7 %all-to-all-done.7 = bf16[1536,8,128]{2,0,1:T(8,128)(2,1)S(1)} async-done(((bf16[1536,8,128]{2,0,1:T(8,128)(2,1)}), bf16[1536,8,128]{2,0,1:T(8,128)(2,1)S(1)}, u32[]{:S(2)}, u32[]{:S(2)}) %all-to-all-start.7) | async-done | bytes 3145760 | tf_op jit(solution)/shard_map/all_to_all | solution.py:108
  388.9 6.1 all-to-all-start.6
  395.5 15.1 %fusion.8 = f32[4,8,40,384]{3,2,1,0:T(8,128)} fusion(bf16[4,384,4096]{2,1,0:T(8,128)(2,1)} %param.15, bf16[8,4,40,4096]{3,2,1,0:T(8,128)(2,1)} %bitcast.257), kind=kOutput, calls=%fused_computation.14 | convolution fusion | flops 4026531840 | bytes 25034752 | tf_op jit(solution)/shard_map/bsecd,efd->bsecf/dot_general | solution.py:65
  410.6 15.3 %fusion.30 = bf16[1,8,4,40,384]{4,3,1,2,0:T(8,128)(2,1)} fusion(f32[4,8,40,384]{3,2,1,0:T(8,128)} %fusion.8, bf16[4,384,4096]{2,1,0:T(8,128)(2,1)} %param.16, bf16[8,4,40,4096]{3,2,1,0:T(8,128)(2,1)} %bitcast.258), kind=kOutput, calls=%fused_computation.42 | convolution fusion | flops 4029480960 | bytes 26017792 | tf_op jit(solution)/shard_map/bsecd,efd->bsecf/dot_general | solution.py:68
  425.9 4.5 gather_fusion.1
  430.4 3.9 select_bitcast_fusion.2
  434.3 29.1 %all-to-all-done.6 = bf16[384,8,512]{2,0,1:T(8,128)(2,1)S(1)} async-done(((bf16[384,8,512]{2,0,1:T(8,128)(2,1)}), bf16[384,8,512]{2,0,1:T(8,128)(2,1)S(1)}, u32[]{:S(2)}, u32[]{:S(2)}) %all-to-all-start.6) | async-done | bytes 3145760 | tf_op jit(solution)/shard_map/all_to_all | solution.py:115
  465.0 6.8 all-to-all-start.8
  472.0 14.2 %fusion.10 = f32[4,8,40,384]{3,2,1,0:T(8,128)S(1)} fusion(bf16[4,384,4096]{2,1,0:T(8,128)(2,1)} %param.15, bf16[8,4,40,4096]{3,2,1,0:T(8,128)(2,1)} %bitcast.259), kind=kOutput, calls=%fused_computation.16 | convolution fusion | flops 4026531840 | bytes 25034752 | tf_op jit(solution)/shard_map/bsecd,efd->bsecf/dot_general | solution.py:65
  486.2 15.0 %fusion.31 = bf16[1,8,4,40,384]{4,3,1,2,0:T(8,128)(2,1)} fusion(f32[4,8,40,384]{3,2,1,0:T(8,128)S(1)} %fusion.10, bf16[4,384,4096]{2,1,0:T(8,128)(2,1)} %param.16, bf16[8,4,40,4096]{3,2,1,0:T(8,128)(2,1)} %bitcast.260), kind=kOutput, calls=%fused_computation.44 | convolution fusion | flops 4029480960 | bytes 26017792 | tf_op jit(solution)/shard_map/bsecd,efd->bsecf/dot_general | solution.py:68
  501.3 10.0 %convert_bitcast_fusion = bf16[1,8,4,40,1024]{4,3,1,2,0:T(8,128)(2,1)S(1)} fusion(bf16[4,1536,1024]{2,1,0:T(8,128)(2,1)} %param.17, bf16[1,8,4,40,1536]{4,3,1,2,0:T(8,128)(2,1)} %all-gather.11.cloned.1.call-done), kind=kOutput, calls=%fused_computation.37 | convolution fusion | flops 4027842560 | bytes 19136512 | tf_op jit(solution)/shard_map/bsecf,efd->bsecd/dot_general | solution.py:72
  511.3 1.8 copy.113
  513.1 26.5 %all-to-all-done.8 = bf16[1536,8,128]{2,0,1:T(8,128)(2,1)} async-done(((bf16[1536,8,128]{2,0,1:T(8,128)(2,1)}), bf16[1536,8,128]{2,0,1:T(8,128)(2,1)}, u32[]{:S(2)}, u32[]{:S(2)}) %all-to-all-start.8) | async-done | bytes 3145760 | tf_op jit(solution)/shard_map/all_to_all | solution.py:116
  539.6 6.4 all-to-all-start.3
  546.0 10.0 %convert_bitcast_fusion.1 = bf16[1,8,4,40,1024]{4,3,1,2,0:T(8,128)(2,1)S(1)} fusion(bf16[4,1536,1024]{2,1,0:T(8,128)(2,1)} %param.17, bf16[1,8,4,40,1536]{4,3,1,2,0:T(8,128)(2,1)} %all-gather.7.cloned.1.call-done), kind=kOutput, calls=%fused_computation.38 | convolution fusion | flops 4027842560 | bytes 19136512 | tf_op jit(solution)/shard_map/bsecf,efd->bsecd/dot_general | solution.py:72
  556.1 1.8 copy.100
  557.8 45.3 %all-to-all-done.3 = bf16[1,8,160,1024]{3,2,0,1:T(8,128)(2,1)S(1)} async-done(((bf16[1,8,160,1024]{3,2,0,1:T(8,128)(2,1)}), bf16[1,8,160,1024]{3,2,0,1:T(8,128)(2,1)S(1)}, u32[]{:S(2)}, u32[]{:S(2)}) %all-to-all-start.3) | async-done | bytes 2621472 | tf_op jit(solution)/shard_map/all_to_all | solution.py:79
  603.2 6.7 all-to-all-start.1
  611.5 3.0 constant_dynamic-slice_fusion.1
  618.3 2.4 collective-permute-start.3
  622.1 1.8 bitcast_dynamic-update-slice_fusion.7
  623.9 16.1 %collective-permute-done = bf16[384,1,512]{2,0,1:T(8,128)(2,1)} collective-permute-done((bf16[384,1,512]{2,0,1:T(8,128)(2,1)}, bf16[384,1,512]{2,0,1:T(8,128)(2,1)}, u32[]{:S(2)}, u32[]{:S(2)}) %collective-permute-start) | collective-permute-done | bytes 393248 | tf_op jit(solution)/shard_map/ppermute | solution.py:27
  640.0 6.4 collective-permute-start.5
  646.4 1.8 bitcast_dynamic-update-slice_fusion.6
  648.1 15.1 %collective-permute-done.1 = bf16[384,1,512]{2,0,1:T(8,128)(2,1)} collective-permute-done((bf16[384,1,512]{2,0,1:T(8,128)(2,1)}, bf16[384,1,512]{2,0,1:T(8,128)(2,1)}, u32[]{:S(2)}, u32[]{:S(2)}) %collective-permute-start.1) | collective-permute-done | bytes 393248 | tf_op jit(solution)/shard_map/ppermute | solution.py:27
  663.2 3.1 collective-permute-start.6
  666.3 1.8 bitcast_dynamic-update-slice_fusion.5
  668.1 4.7 collective-permute-done.2
  673.5 35.2 %collective-permute-done.3 = bf16[384,1,512]{2,0,1:T(8,128)(2,1)S(1)} collective-permute-done((bf16[384,1,512]{2,0,1:T(8,128)(2,1)}, bf16[384,1,512]{2,0,1:T(8,128)(2,1)S(1)}, u32[]{:S(2)}, u32[]{:S(2)}) %collective-permute-start.3) | collective-permute-done | bytes 393248 | tf_op jit(solution)/shard_map/ppermute | solution.py:27
  709.5 7.7 collective-permute-done.4
  717.9 10.4 %collective-permute-done.5 = bf16[384,1,512]{2,0,1:T(8,128)(2,1)S(1)} collective-permute-done((bf16[384,1,512]{2,0,1:T(8,128)(2,1)S(1)}, bf16[384,1,512]{2,0,1:T(8,128)(2,1)S(1)}, u32[]{:S(2)}, u32[]{:S(2)}) %collective-permute-start.5) | collective-permute-done | bytes 393248 | tf_op jit(solution)/shard_map/ppermute | solution.py:27
  729.1 6.7 collective-permute-done.6
  736.6 4.3 gather_fusion
  740.9 4.6 copy.118
  745.5 4.6 copy.125
  750.1 4.6 copy.121
  754.8 4.6 copy.126
  759.4 4.6 copy.124
  764.0 4.6 copy.127
  768.7 5.4 gather_fusion.3
  774.1 8.2 %gather_fusion.2 = bf16[1024,1024]{1,0:T(8,128)(2,1)} fusion(bf16[1280,1024]{1,0:T(8,128)(2,1)} %bitcast.32, s32[1024]{0:T(1024)S(1)} %broadcast_clamp_fusion.1), kind=kCustom, calls=%fused_computation.clone | custom fusion | bytes 4198400 | tf_op jit(solution)/shard_map/jit(take_along_axis)/gather | solution.py:82
  (103 shorter events, 28.0 us)
Async XLA Ops:
  7.2 23.3 %copy-start.5 = (bf16[2,128,1024]{2,1,0:T(8,128)(2,1)S(1)}, bf16[2,128,1024]{2,1,0:T(8,128)(2,1)}, u32[]{:S(2)}) copy-start(bf16[2,128,1024]{2,1,0:T(8,128)(2,1)} %param.12) | copy-start | bytes 1572868
  7.2 388.3 %all-gather.9.cloned.1.call-start = ((), (), s32[]{:S(2)}) async-start(), calls=%async_computation.11 | async-start | bytes 13107200 | tf_op jit(solution)/shard_map/all_gather | solution.py:63
  100.2 5.4 copy-start.9
  100.2 5.4 copy-start.10
  100.2 61.6 %all-to-all-start = ((bf16[1,8,160,1024]{3,2,0,1:T(8,128)(2,1)}), bf16[1,8,160,1024]{3,2,0,1:T(8,128)(2,1)}, u32[]{:S(2)}, u32[]{:S(2)}) async-start(bf16[1,8,160,1024]{3,2,0,1:T(8,128)(2,1)} %bitcast.8), calls=%async_computation | async-start | bytes 5242880 | tf_op jit(solution)/shard_map/all_to_all | solution.py:62
  161.8 74.6 %all-to-all-start.5 = ((bf16[384,8,512]{2,0,1:T(8,128)(2,1)}), bf16[384,8,512]{2,0,1:T(8,128)(2,1)S(1)}, u32[]{:S(2)}, u32[]{:S(2)}) async-start(bf16[384,8,512]{2,0,1:T(8,128)(2,1)} %copy.120), calls=%async_computation.5 | async-start | bytes 6291456 | tf_op jit(solution)/shard_map/all_to_all | solution.py:107
  168.0 304.1 %all-gather.5.cloned.1.call-start = ((), (), s32[]{:S(2)}) async-start(), calls=%async_computation.9 | async-start | bytes 13107200 | tf_op jit(solution)/shard_map/all_gather | solution.py:63
  236.4 1.7 copy-start.2
  238.1 74.5 %all-to-all-start.4 = ((bf16[384,8,512]{2,0,1:T(8,128)(2,1)}), bf16[384,8,512]{2,0,1:T(8,128)(2,1)}, u32[]{:S(2)}, u32[]{:S(2)}) async-start(bf16[384,8,512]{2,0,1:T(8,128)(2,1)} %copy.117), calls=%async_computation.4 | async-start | bytes 6291456 | tf_op jit(solution)/shard_map/all_to_all | solution.py:106
  312.6 74.6 %all-to-all-start.7 = ((bf16[1536,8,128]{2,0,1:T(8,128)(2,1)}), bf16[1536,8,128]{2,0,1:T(8,128)(2,1)S(1)}, u32[]{:S(2)}, u32[]{:S(2)}) async-start(bf16[1536,8,128]{2,0,1:T(8,128)(2,1)} %copy.123), calls=%async_computation.7 | async-start | bytes 6291456 | tf_op jit(solution)/shard_map/all_to_all | solution.py:108
  387.2 1.7 copy-start.1
  388.9 74.5 %all-to-all-start.6 = ((bf16[384,8,512]{2,0,1:T(8,128)(2,1)}), bf16[384,8,512]{2,0,1:T(8,128)(2,1)S(1)}, u32[]{:S(2)}, u32[]{:S(2)}) async-start(bf16[384,8,512]{2,0,1:T(8,128)(2,1)} %get-tuple-element.41), calls=%async_computation.6 | async-start | bytes 6291456 | tf_op jit(solution)/shard_map/all_to_all | solution.py:115
  395.0 106.3 %all-gather.11.cloned.1.call-start = ((), (), s32[]{:S(2)}) async-start(), calls=%async_computation.12 | async-start | bytes 4915200 | tf_op jit(solution)/shard_map/all_gather | solution.py:74
  463.4 1.6 copy-start
  465.0 74.5 %all-to-all-start.8 = ((bf16[1536,8,128]{2,0,1:T(8,128)(2,1)}), bf16[1536,8,128]{2,0,1:T(8,128)(2,1)}, u32[]{:S(2)}, u32[]{:S(2)}) async-start(bf16[1536,8,128]{2,0,1:T(8,128)(2,1)} %select_bitcast_fusion.2), calls=%async_computation.8 | async-start | bytes 6291456 | tf_op jit(solution)/shard_map/all_to_all | solution.py:116
  471.8 74.2 %all-gather.7.cloned.1.call-start = ((), (), s32[]{:S(2)}) async-start(), calls=%async_computation.10 | async-start | bytes 4915200 | tf_op jit(solution)/shard_map/all_gather | solution.py:74
  539.6 63.6 %all-to-all-start.3 = ((bf16[1,8,160,1024]{3,2,0,1:T(8,128)(2,1)}), bf16[1,8,160,1024]{3,2,0,1:T(8,128)(2,1)S(1)}, u32[]{:S(2)}, u32[]{:S(2)}) async-start(bf16[1,8,160,1024]{3,2,0,1:T(8,128)(2,1)} %bitcast.245), calls=%async_computation.3 | async-start | bytes 5242880 | tf_op jit(solution)/shard_map/all_to_all | solution.py:79
  557.8 53.0 %copy-start.6 = (f32[2,128,8]{1,2,0:T(8,128)S(1)}, f32[2,128,8]{1,2,0:T(8,128)}, u32[]{:S(2)}) copy-start(f32[2,128,8]{1,2,0:T(8,128)} %param.14) | copy-start | bytes 24580
  603.2 170.9 %all-to-all-start.1 = ((bf16[1,8,160,1024]{3,2,0,1:T(8,128)(2,1)}), bf16[1,8,160,1024]{3,2,0,1:T(8,128)(2,1)}, u32[]{:S(2)}, u32[]{:S(2)}) async-start(bf16[1,8,160,1024]{3,2,0,1:T(8,128)(2,1)} %bitcast.243), calls=%async_computation.1 | async-start | bytes 5242880 | tf_op jit(solution)/shard_map/all_to_all | solution.py:79
  614.5 25.5 %collective-permute-start = (bf16[384,1,512]{2,0,1:T(8,128)(2,1)}, bf16[384,1,512]{2,0,1:T(8,128)(2,1)}, u32[]{:S(2)}, u32[]{:S(2)}) collective-permute-start(bf16[384,1,512]{2,0,1:T(8,128)(2,1)} %get-tuple-element.32), channel_id=1, source_target_pairs={{0,4},{4,0},{8,12},{12,8},{16,20},{20,16},{24,28},{28,24},{1,5},{5... | collective-permute-start | bytes 1179656 | tf_op jit(solution)/shard_map/ppermute | solution.py:27
  616.0 47.3 %collective-permute-start.1 = (bf16[384,1,512]{2,0,1:T(8,128)(2,1)}, bf16[384,1,512]{2,0,1:T(8,128)(2,1)}, u32[]{:S(2)}, u32[]{:S(2)}) collective-permute-start(bf16[384,1,512]{2,0,1:T(8,128)(2,1)} %get-tuple-element.31), channel_id=1, source_target_pairs={{0,8},{4,12},{8,0},{12,4},{16,24},{20,28},{24,16},{28,20},{1,9},{5... | collective-permute-start | bytes 1179656 | tf_op jit(solution)/shard_map/ppermute | solution.py:27
  616.8 55.9 %collective-permute-start.2 = (bf16[384,1,512]{2,0,1:T(8,128)(2,1)}, bf16[384,1,512]{2,0,1:T(8,128)(2,1)S(1)}, u32[]{:S(2)}, u32[]{:S(2)}) collective-permute-start(bf16[384,1,512]{2,0,1:T(8,128)(2,1)} %get-tuple-element.30), channel_id=1, source_target_pairs={{0,12},{4,8},{8,4},{12,0},{16,28},{20,24},{24,20},{28,16},{1,13},{... | collective-permute-start | bytes 1179656 | tf_op jit(solution)/shard_map/ppermute | solution.py:27
  618.3 90.4 %collective-permute-start.3 = (bf16[384,1,512]{2,0,1:T(8,128)(2,1)}, bf16[384,1,512]{2,0,1:T(8,128)(2,1)S(1)}, u32[]{:S(2)}, u32[]{:S(2)}) collective-permute-start(bf16[384,1,512]{2,0,1:T(8,128)(2,1)} %get-tuple-element.29), channel_id=1, source_target_pairs={{0,16},{4,20},{8,24},{12,28},{16,0},{20,4},{24,8},{28,12},{1,17},{... | collective-permute-start | bytes 1179656 | tf_op jit(solution)/shard_map/ppermute | solution.py:27
  620.7 96.5 %collective-permute-start.4 = (bf16[384,1,512]{2,0,1:T(8,128)(2,1)}, bf16[384,1,512]{2,0,1:T(8,128)(2,1)S(1)}, u32[]{:S(2)}, u32[]{:S(2)}) collective-permute-start(bf16[384,1,512]{2,0,1:T(8,128)(2,1)} %get-tuple-element.28), channel_id=1, source_target_pairs={{0,20},{4,16},{8,28},{12,24},{16,4},{20,0},{24,12},{28,8},{1,21},{... | collective-permute-start | bytes 1179656 | tf_op jit(solution)/shard_map/ppermute | solution.py:27
  640.0 88.3 %collective-permute-start.5 = (bf16[384,1,512]{2,0,1:T(8,128)(2,1)S(1)}, bf16[384,1,512]{2,0,1:T(8,128)(2,1)S(1)}, u32[]{:S(2)}, u32[]{:S(2)}) collective-permute-start(bf16[384,1,512]{2,0,1:T(8,128)(2,1)S(1)} %get-tuple-element.27), channel_id=1, source_target_pairs={{0,24},{4,28},{8,16},{12,20},{16,8},{20,12},{24,0},{28,4},{1,25},{... | collective-permute-start | bytes 1179656 | tf_op jit(solution)/shard_map/ppermute | solution.py:27
  663.2 72.6 %collective-permute-start.6 = (bf16[384,1,512]{2,0,1:T(8,128)(2,1)S(1)}, bf16[384,1,512]{2,0,1:T(8,128)(2,1)S(1)}, u32[]{:S(2)}, u32[]{:S(2)}) collective-permute-start(bf16[384,1,512]{2,0,1:T(8,128)(2,1)S(1)} %get-tuple-element.26), channel_id=1, source_target_pairs={{0,28},{4,24},{8,20},{12,16},{16,12},{20,8},{24,4},{28,0},{1,29},{... | collective-permute-start | bytes 1179656 | tf_op jit(solution)/shard_map/ppermute | solution.py:27
  774.1 8.3 %copy-start.3 = (bf16[1024,1024]{1,0:T(8,128)(2,1)S(1)}, bf16[1024,1024]{1,0:T(8,128)(2,1)}, u32[]{:S(2)}) copy-start(bf16[1024,1024]{1,0:T(8,128)(2,1)} %gather_fusion.3) | copy-start | bytes 6291460
  774.1 8.3 %copy-start.7 = (pred[1024]{0:T(1024)(128)(4,1)S(1)}, pred[1024]{0:T(1024)(128)(4,1)}, u32[]{:S(2)}) copy-start(pred[1024]{0:T(1024)(128)(4,1)} %get-tuple-element.24) | copy-start | bytes 3076
  774.1 9.8 %copy-start.8 = (pred[1024]{0:T(1024)(128)(4,1)S(1)}, pred[1024]{0:T(1024)(128)(4,1)}, u32[]{:S(2)}) copy-start(pred[1024]{0:T(1024)(128)(4,1)} %get-tuple-element.22) | copy-start | bytes 3076
  782.3 1.6 copy-start.4
Sparse Core Ops, SparseCore 0:
  96.2 69.6 all-gather.8
  170.3 71.0 all-gather.4
  426.0 33.8 all-gather.10
  501.4 33.8 all-gather.6
